TPU v7x, 256 devices: a whole 4x4x8 slice. The times are simulated.
256 devices in a mesh: ep: 32 (over x, y, core), gd: 8 (over z).
Axes of the slice: x: 4, y: 4, z: 8, core: 2. Of those that a mesh axis runs over, the one named last changes fastest.
Arguments:
- tokens: bfloat16 [2048, 4096], P(('ep', 'gd')), may hold values from -6 to 6
- expert_ids: int32 [2048, 8], P(('ep', 'gd')), may hold values from 0 to 31, all different within a row; in each aligned block of 8 rows (0 to 7, 8 to 15, ...) at most 3 rows name the same one
- combine: float32 [2048, 8], P(('ep', 'gd')), may hold values from 0.02 to 0.3
- w_gate: bfloat16 [32, 4096, 1536], P('ep', None, 'gd'), may hold values from -0.09375 to 0.09375
- w_up: bfloat16 [32, 4096, 1536], P('ep', None, 'gd'), may hold values from -0.09375 to 0.09375
- w_down: bfloat16 [32, 1536, 4096], P('ep', 'gd'), may hold values from -0.15625 to 0.15625
- w_query: bfloat16 [4096, 4096], P(None, 'gd'), may hold values from -0.09375 to 0.09375
- w_key: bfloat16 [4096, 1024], P(None, 'gd'), may hold values from -0.09375 to 0.09375
- w_value: bfloat16 [4096, 1024], P(None, 'gd'), may hold values from -0.09375 to 0.09375
- cache_keys: bfloat16 [2048, 8, 64, 128], P('ep', 'gd'), may hold values from -68 to 68
- cache_values: bfloat16 [2048, 8, 64, 128], P('ep', 'gd'), may hold values from -6 to 6
- lengths: int32 [2048], P('ep'), may hold values from 1 to 64, as said below
Outputs:
- stream: bfloat16 [2048, 4096], P(('ep', 'gd'))
- guard: bfloat16 [2048, 4096], P('ep', 'gd')
Inputs may be any that keep to these rules, and one draw needn't show every extreme that they name: `expert_ids`: each row names 8 different experts; in the rows of one device no expert is named by more than 3 rows. `lengths`: some row has the full window of 64 positions.
All inputs are finite; a program needn't handle non-finite values.
Results may differ from a plain program's by a relative error of at most 0.03.
Values may be sent and summed in bfloat16 or wider, within the bound.
No kernel may reach another device: no remote copies, remote signals or barrier semaphores. Data moves between devices by JAX's collectives and lax.ppermute only.
A program may use at most 128 MiB of HBM per device.

v0:
```python
import math
import jax
import jax.numpy as jnp
from jax import lax
from jax.sharding import PartitionSpec as P

EPSILON = 1e-06


def norm_rows(values):
    widened = values.astype(jnp.float32)
    return (
        widened * lax.rsqrt(jnp.mean(widened * widened, axis=-1, keepdims=True) + EPSILON)
    ).astype(jnp.bfloat16)


def slot_numbers(chosen, experts):
    blocks_n, rows_n, picks_n = chosen.shape
    flat_ids = chosen.reshape(blocks_n, rows_n * picks_n)
    onehot = (flat_ids[:, :, None] == jnp.arange(experts, dtype=jnp.int32)[None, None, :]).astype(
        jnp.int32
    )
    before = jnp.cumsum(onehot, axis=1) - onehot
    return jnp.sum(before * onehot, axis=-1).reshape(blocks_n, rows_n, picks_n)


def build_slots(row_blocks, targets, slots_n):
    wanted = jnp.any(
        targets[:, None, :, :] == jnp.arange(slots_n, dtype=jnp.int32)[None, :, None, None], axis=-1
    )
    selector = wanted.astype(jnp.bfloat16)
    return jnp.einsum(
        "bsr,brd->bsd", selector, row_blocks, preferred_element_type=jnp.float32
    ).astype(jnp.bfloat16)


def per_device(
    tokens,
    expert_ids,
    combine,
    w_gate,
    w_up,
    w_down,
    w_query,
    w_key,
    w_value,
    cache_keys,
    cache_values,
    lengths,
):
    rows_n, width = tokens.shape
    picks_n = expert_ids.shape[1]
    experts = lax.axis_size("ep")
    members = lax.axis_size("gd")
    capacity = max(2, 3 * rows_n * picks_n // (2 * experts))
    slots_n = experts * capacity
    normed = norm_rows(tokens)
    own_slot = slot_numbers(expert_ids[None], experts)[0]
    own_dest = expert_ids * capacity + own_slot
    group_normed, group_ids = (
        lax.all_gather(normed, "gd", axis=0, tiled=True),
        lax.all_gather(expert_ids, "gd", axis=0, tiled=True),
    )
    group_ids = group_ids.reshape(members, rows_n, picks_n)
    group_dest = group_ids * capacity + slot_numbers(group_ids, experts)
    outgoing = build_slots(group_normed.reshape(members, rows_n, width), group_dest, slots_n)
    outgoing = outgoing.reshape(members, experts, capacity, width)
    arrived = lax.all_to_all(outgoing, "ep", split_axis=1, concat_axis=1, tiled=True)
    slot_rows = arrived.reshape(-1, width)
    gate_val = jnp.dot(slot_rows, w_gate[0], preferred_element_type=jnp.float32)
    up_val = jnp.dot(slot_rows, w_up[0], preferred_element_type=jnp.float32)
    active = (jax.nn.silu(gate_val) * up_val).astype(jnp.bfloat16)
    partial_out = jnp.dot(active, w_down[0], preferred_element_type=jnp.float32).astype(
        jnp.bfloat16
    )
    summed = lax.psum_scatter(
        lax.optimization_barrier(partial_out).astype(jnp.float32).astype(jnp.bfloat16),
        "gd",
        scatter_dimension=0,
        tiled=True,
    ).astype(jnp.float32)
    returned = lax.all_to_all(
        summed.reshape(experts, capacity, width), "ep", split_axis=0, concat_axis=0, tiled=True
    )
    matches = own_dest[:, :, None] == jnp.arange(slots_n, dtype=jnp.int32)[None, None, :]
    weight_rows = jnp.sum(jnp.where(matches, combine[:, :, None], 0.0), axis=1)
    mixture = jnp.dot(
        weight_rows,
        returned.reshape(slots_n, width),
        precision=lax.Precision.HIGHEST,
        preferred_element_type=jnp.float32,
    )
    stream = (tokens.astype(jnp.float32) + mixture).astype(jnp.bfloat16)
    group_stream = lax.all_gather(stream, "gd", axis=0, tiled=True)
    guard_norm = norm_rows(group_stream)
    queries = jnp.dot(guard_norm, w_query, preferred_element_type=jnp.float32)
    key_new = jnp.dot(guard_norm, w_key, preferred_element_type=jnp.float32).astype(jnp.bfloat16)
    value_new = jnp.dot(guard_norm, w_value, preferred_element_type=jnp.float32).astype(
        jnp.bfloat16
    )
    group_total, heads_kv, window_len, head_size = cache_keys.shape
    heads_per = w_query.shape[1] // (heads_kv * head_size)
    queries = queries.reshape(group_total, heads_kv, heads_per, head_size)
    key_new = key_new.reshape(group_total, heads_kv, head_size)
    value_new = value_new.reshape(group_total, heads_kv, head_size)
    scale_factor = 1.0 / math.sqrt(head_size)
    scores = (
        jnp.einsum(
            "rhgd,rhjd->rhgj",
            queries,
            cache_keys.astype(jnp.float32),
            precision=lax.Precision.HIGHEST,
        )
        * scale_factor
    )
    own_score = (
        jnp.einsum(
            "rhgd,rhd->rhg", queries, key_new.astype(jnp.float32), precision=lax.Precision.HIGHEST
        )
        * scale_factor
    )
    positions = jnp.arange(window_len, dtype=jnp.int32)
    allowed = positions[None, None, None, :] >= (window_len - lengths)[:, None, None, None]
    masked = jnp.where(allowed, scores, -jnp.inf)
    highest = jnp.maximum(jnp.max(masked, axis=-1), own_score)
    weights = jnp.exp(masked - highest[..., None])
    own_weight = jnp.exp(own_score - highest)
    denominator = jnp.sum(weights, axis=-1) + own_weight
    probabilities = weights / denominator[..., None]
    own_prob = own_weight / denominator
    attended = jnp.einsum(
        "rhgj,rhjd->rhgd",
        probabilities,
        cache_values.astype(jnp.float32),
        precision=lax.Precision.HIGHEST,
    )
    attended = attended + own_prob[..., None] * value_new.astype(jnp.float32)[:, :, None, :]
    guard = attended.astype(jnp.bfloat16).reshape(group_total, heads_kv * heads_per * head_size)
    return (stream, guard)


def solution(mesh):
    return jax.shard_map(
        per_device,
        mesh=mesh,
        in_specs=(
            P(("ep", "gd"), None),
            P(("ep", "gd"), None),
            P(("ep", "gd"), None),
            P("ep", None, "gd"),
            P("ep", None, "gd"),
            P("ep", "gd", None),
            P(None, "gd"),
            P(None, "gd"),
            P(None, "gd"),
            P("ep", "gd", None, None),
            P("ep", "gd", None, None),
            P("ep"),
        ),
        out_specs=(P(("ep", "gd"), None), P("ep", "gd")),
        check_vma=False,
    )
```

profile of v0, /device:TPU:32, one launch (start us, length us, event | category | flops | bytes accessed | tf_op | source)
XLA Modules:
  0.0 350.0 jit_solution(959510672783072410)
XLA Ops:
  7.2 0.0 copy-start
  7.2 0.0 reduce-scatter.2.cloned.1.call-start
  7.2 27.5 %all_gather.9 = s32[64,8]{1,0:T(8,128)S(1)} all-gather(s32[8,8]{1,0:T(8,128)} %param.13), channel_id=1, replica_groups=mesh['ep'=32,'gd'=8] {'gd'}, dimensions={0}, use_global_device_ids=true | all-gather | bytes 2304 | tf_op jit(solution)/shard_map/all_gather | solution.py:62
  34.7 0.1 eq.75
  34.8 0.1 copy.23
  34.9 1.4 fusion.49
  36.2 0.1 copy.24
  36.3 0.1 copy.25
  36.4 0.2 fusion.31
  36.6 1.0 fusion.33
  37.6 0.9 fusion.34
  38.5 25.2 %all_gather.10 = bf16[64,4096]{1,0:T(8,128)(2,1)S(1)} all-gather(bf16[8,4096]{1,0:T(8,128)(2,1)S(1)} %fusion.34), channel_id=1, replica_groups=mesh['ep'=32,'gd'=8] {'gd'}, dimensions={0}, use_global_device_ids=true | all-gather | bytes 589824 | tf_op jit(solution)/shard_map/all_gather | solution.py:61
  63.7 1.8 convolution_convert_fusion.1
  65.6 3.4 copy.26
  69.0 80.2 %all_to_all.10 = bf16[8,32,3,4096]{3,0,2,1:T(8,128)(2,1)} all-to-all(bf16[8,32,3,4096]{3,0,2,1:T(8,128)(2,1)S(1)} %bitcast.49), channel_id=1, replica_groups=mesh['ep'=32,'gd'=8] {'ep'}, dimensions={1} | all-to-all | bytes 12582912 | tf_op jit(solution)/shard_map/all_to_all | solution.py:68
  149.2 11.4 %copy.27 = bf16[8,32,3,4096]{3,2,1,0:T(4,128)(2,1)} copy(bf16[8,32,3,4096]{3,0,2,1:T(8,128)(2,1)} %all_to_all.10) | data formatting | bytes 12582912 | tf_op jit(solution)/shard_map/all_to_all | solution.py:68
  160.7 0.0 copy-start.6
  160.7 13.9 %reshape.239 = bf16[768,4096]{1,0:T(8,128)(2,1)} reshape(bf16[8,32,3,4096]{3,2,1,0:T(4,128)(2,1)} %copy.27) | data formatting | bytes 12582912 | tf_op jit(solution)/shard_map/reshape | solution.py:69
  174.5 0.0 copy-done.6
  174.5 5.8 %fusion.4 = f32[768,192]{0,1:T(8,128)} fusion(bf16[768,4096]{1,0:T(8,128)(2,1)} %reshape.239, bf16[1,4096,192]{1,2,0:T(8,128)(2,1)S(1)} %copy-done.6), kind=kOutput, calls=%fused_computation.7 | convolution fusion | flops 1207959552 | bytes 8454144 | tf_op jit(solution)/shard_map/dot_general | solution.py:70
  180.3 0.0 copy-done
  180.3 13.3 %convolution_convert_fusion = bf16[768,4096]{1,0:T(8,128)(2,1)} fusion(bf16[1,192,4096]{2,1,0:T(8,128)(2,1)S(1)} %copy-done, bf16[768,4096]{1,0:T(8,128)(2,1)} %reshape.239, bf16[1,4096,192]{1,2,0:T(8,128)(2,1)} %param.16, f32[768,192]{0,1:T(8,128)} %fusion.4), kind=kOutput, calls=%fused_computation | convolution fusion | flops 2419949568 | bytes 16318464 | tf_op jit(solution)/shard_map/dot_general | solution.py:73
  193.7 0.0 reduce-scatter.2.cloned.1.call-update
  193.7 0.0 copy-start.4
  193.7 0.0 copy-start.5
  193.7 0.0 copy-start.8
  193.7 70.1 %reduce-scatter.2.cloned.1.call-done = bf16[96,4096]{1,0:T(8,128)(2,1)} async-done(((bf16[768,4096]{1,0:T(8,128)(2,1)}), bf16[96,4096]{1,0:T(8,128)(2,1)}) %reduce-scatter.2.cloned.1.call-update) | async-done | bytes 786448 | tf_op jit(solution)/shard_map/reduce_scatter | solution.py:76
  263.8 2.8 reshape.248
  266.6 0.0 copy-start.2
  266.6 7.6 %all-to-all-start.1 = ((f32[32,3,4096]{2,1,0:T(4,128)}), f32[32,3,4096]{2,1,0:T(4,128)}, u32[]{:S(2)}, u32[]{:S(2)}) async-start(f32[32,3,4096]{2,1,0:T(4,128)} %reshape.248), calls=%async_computation.2 | async-start | bytes 4194304 | tf_op jit(solution)/shard_map/all_to_all | solution.py:82
  274.2 0.0 copy-done.4
  274.2 0.1 eq.68
  274.3 0.1 fusion.39
  274.4 0.1 reduce_window_sum.22
  274.4 0.2 select_reduce_fusion.1
  274.6 0.1 squeeze_reshape.3
  274.7 0.0 copy-done.5
  274.7 0.1 select_reduce_fusion
  274.8 0.0 copy-done.8
  274.9 0.1 iota_compare_fusion.3
  274.9 27.9 %all-to-all-done.1 = f32[32,3,4096]{2,1,0:T(4,128)} async-done(((f32[32,3,4096]{2,1,0:T(4,128)}), f32[32,3,4096]{2,1,0:T(4,128)}, u32[]{:S(2)}, u32[]{:S(2)}) %all-to-all-start.1) | async-done | bytes 1572896 | tf_op jit(solution)/shard_map/all_to_all | solution.py:82
  302.9 2.0 reshape.242
  304.9 0.0 copy-done.2
  304.9 0.8 fusion
  305.8 0.0 copy-start.3
  305.8 0.0 copy-start.1
  305.8 26.7 %all_gather.11 = bf16[64,4096]{1,0:T(8,128)(2,1)S(1)} all-gather(bf16[8,4096]{1,0:T(8,128)(2,1)S(1)} %fusion), channel_id=1, replica_groups=mesh['ep'=32,'gd'=8] {'gd'}, dimensions={0}, use_global_device_ids=true | all-gather | bytes 589824 | tf_op jit(solution)/shard_map/all_gather | solution.py:94
  332.5 0.2 fusion.18
  332.8 3.1 fusion.47
  335.9 0.0 copy-done.1
  335.9 0.0 copy-start.7
  335.9 0.3 fusion.17
  336.3 0.4 fusion.40
  336.6 3.0 fusion.50
  339.7 0.0 copy-done.3
  339.7 0.2 fusion.36
  339.9 1.6 fusion.16
  341.5 0.0 copy-done.7
  341.5 1.0 fusion.15
  342.5 0.6 copy.34
  (9 shorter events, 0.1 us)
Async XLA Ops:
  7.2 173.2 %copy-start = (bf16[1,192,4096]{2,1,0:T(8,128)(2,1)S(1)}, bf16[1,192,4096]{2,1,0:T(8,128)(2,1)}, u32[]{:S(2)}) copy-start(bf16[1,192,4096]{2,1,0:T(8,128)(2,1)} %param.17) | copy-start | bytes 4718596
  7.2 256.6 %reduce-scatter.2.cloned.1.call-start = ((), (), s32[]{:S(2)}) async-start(), calls=%async_computation.3 | async-start | bytes 7077888 | tf_op jit(solution)/shard_map/reduce_scatter | solution.py:76
  160.7 13.9 %copy-start.6 = (bf16[1,4096,192]{1,2,0:T(8,128)(2,1)S(1)}, bf16[1,4096,192]{1,2,0:T(8,128)(2,1)}, u32[]{:S(2)}) copy-start(bf16[1,4096,192]{1,2,0:T(8,128)(2,1)} %param.15) | copy-start | bytes 4718596
  193.7 80.5 %copy-start.4 = (s32[8,8]{1,0:T(8,128)S(1)}, s32[8,8]{1,0:T(8,128)}, u32[]{:S(2)}) copy-start(s32[8,8]{1,0:T(8,128)} %param.13) | copy-start | bytes 772
  193.7 81.0 %copy-start.5 = (f32[8,8]{1,0:T(8,128)S(1)}, f32[8,8]{1,0:T(8,128)}, u32[]{:S(2)}) copy-start(f32[8,8]{1,0:T(8,128)} %param.14) | copy-start | bytes 772
  193.7 81.1 %copy-start.8 = (s32[64]{0:T(128)S(1)}, s32[64]{0:T(128)}, u32[]{:S(2)}) copy-start(s32[64]{0:T(128)} %param.23) | copy-start | bytes 772
  266.6 38.3 %copy-start.2 = (bf16[8,4096]{1,0:T(8,128)(2,1)S(1)}, bf16[8,4096]{1,0:T(8,128)(2,1)}, u32[]{:S(2)}) copy-start(bf16[8,4096]{1,0:T(8,128)(2,1)} %param.12) | copy-start | bytes 196612
  266.6 36.3 %all-to-all-start.1 = ((f32[32,3,4096]{2,1,0:T(4,128)}), f32[32,3,4096]{2,1,0:T(4,128)}, u32[]{:S(2)}, u32[]{:S(2)}) async-start(f32[32,3,4096]{2,1,0:T(4,128)} %reshape.248), calls=%async_computation.2 | async-start | bytes 4194304 | tf_op jit(solution)/shard_map/all_to_all | solution.py:82
  305.8 33.9 %copy-start.3 = (bf16[8,4096]{1,0:T(8,128)(2,1)}, bf16[8,4096]{1,0:T(8,128)(2,1)S(1)}, u32[]{:S(2)}) copy-start(bf16[8,4096]{1,0:T(8,128)(2,1)S(1)} %fusion) | copy-start | bytes 196612
  305.8 30.1 %copy-start.1 = (bf16[4096,128]{1,0:T(8,128)(2,1)S(1)}, bf16[4096,128]{1,0:T(8,128)(2,1)}, u32[]{:S(2)}) copy-start(bf16[4096,128]{1,0:T(8,128)(2,1)} %param.19) | copy-start | bytes 3145732
  335.9 5.6 %copy-start.7 = (bf16[64,1,64,128]{3,2,1,0:T(8,128)(2,1)S(1)}, bf16[64,1,64,128]{3,2,1,0:T(8,128)(2,1)}, u32[]{:S(2)}) copy-start(bf16[64,1,64,128]{3,2,1,0:T(8,128)(2,1)} %param.22) | copy-start | bytes 3145732
Sparse Core Ops, SparseCore 0:
  193.8 69.9 reduce-scatter.1
where the time goes:
time: 351 us; the launch traced here: 350 us
  blocking collectives  160 us (46%)
  waiting for transfers between devices  98 us (28%)
  local copies, waits for them, and re-layouts  34.8 us (10%)
  matrix products  31.2 us (9%)
  between operations  14.3 us (4%)
  starting transfers between devices  7.61 us (2%)
  other arithmetic  4.49 us (1%)
    all_to_all x1, blocking collectives, per_device(): lax.all_to_all(outgoing, 'ep', split_axis=1, concat_axis=1, tiled=True)  80.2 us
    reduce_scatter x1, waiting for transfers between devices, per_device(): lax.psum_scatter(lax.optimization_barrier(partial_out).astype(jnp.float32...  70.1 us
    all_to_all x1, waiting for transfers between devices, per_device(): lax.all_to_all(summed.reshape(experts, capacity, width), 'ep', split_axis...  27.9 us
    all_gather x1, blocking collectives, per_device(): lax.all_gather(expert_ids, 'gd', axis=0, tiled=True)  27.5 us
    all_gather x1, blocking collectives, per_device(): group_stream = lax.all_gather(stream, 'gd', axis=0, tiled=True)  26.7 us
    all_gather x1, blocking collectives, per_device(): lax.all_gather(normed, 'gd', axis=0, tiled=True)  25.2 us
    reshape x1, local copies, waits for them, and re-layouts, per_device(): slot_rows = arrived.reshape(-1, width)  13.9 us
    dot_general x1, matrix products, per_device(): jnp.dot(active, w_down[0], preferred_element_type=jnp.float32)  13.3 us
  transfers between devices with their start and end apart: 2, of which 2 were waited for; matrix products, arithmetic and copies ran while one was open for 0% of the time, Pallas kernels for 0%

commit v1 on v0

--- a/solution.py
+++ b/solution.py
@@ -91,7 +91,9 @@
         preferred_element_type=jnp.float32,
     )
     stream = (tokens.astype(jnp.float32) + mixture).astype(jnp.bfloat16)
-    group_stream = lax.all_gather(stream, "gd", axis=0, tiled=True)
+    group_stream = jnp.concatenate(
+        lax.all_to_all(jnp.stack([stream] * lax.axis_size("gd")), "gd", 0, 0), axis=0
+    )
     guard_norm = norm_rows(group_stream)
     queries = jnp.dot(guard_norm, w_query, preferred_element_type=jnp.float32)
     key_new = jnp.dot(guard_norm, w_key, preferred_element_type=jnp.float32).astype(jnp.bfloat16)

time: 351 us -> 348 us (level)
  blocking collectives: 160 us -> 133 us
  waiting for transfers between devices: 98 us -> 107 us
  local copies, waits for them, and re-layouts: 34.8 us -> 42.1 us
  starting transfers between devices: 7.61 us -> 14.2 us
    all_gather x1 -> x0, blocking collectives: 26.7 us -> none  [per_device(): group_stream = lax.all_gather(stream, 'gd', axis=0, tiled=True)]
    all_to_all x0 -> x1, waiting for transfers between devices: none -> 9.33 us  [per_device(): lax.all_to_all(jnp.stack([stream] * lax.axis_size('gd')), 'gd', 0, 0)]
    another operation x1 -> x2, local copies, waits for them, and re-layouts: 0.05 us -> 7.25 us
    all_to_all x0 -> x1, starting transfers between devices: none -> 6.57 us  [per_device(): lax.all_to_all(jnp.stack([stream] * lax.axis_size('gd')), 'gd', 0, 0)]
  transfers between devices with their start and end apart: 2 -> 3, of which waited for: 2 -> 3; matrix products, arithmetic and copies ran while one was open for 0% -> 2% of each run, Pallas kernels for 0% -> 0%
where the time goes in v1:
time: 348 us; the launch traced here: 345 us
  blocking collectives  133 us (38%)
  waiting for transfers between devices  107 us (31%)
  local copies, waits for them, and re-layouts  42.1 us (12%)
  matrix products  29.5 us (8%)
  between operations  14.3 us (4%)
  starting transfers between devices  14.2 us (4%)
  other arithmetic  4.47 us (1%)
    all_to_all x1, blocking collectives, per_device(): lax.all_to_all(outgoing, 'ep', split_axis=1, concat_axis=1, tiled=True)  80.2 us
    reduce_scatter x1, waiting for transfers between devices, per_device(): lax.psum_scatter(lax.optimization_barrier(partial_out).astype(jnp.float32...  70.1 us
    all_to_all x1, waiting for transfers between devices, per_device(): lax.all_to_all(summed.reshape(experts, capacity, width), 'ep', split_axis...  28 us
    all_gather x1, blocking collectives, per_device(): lax.all_gather(expert_ids, 'gd', axis=0, tiled=True)  27.5 us
    all_gather x1, blocking collectives, per_device(): lax.all_gather(normed, 'gd', axis=0, tiled=True)  25.2 us
    reshape x1, local copies, waits for them, and re-layouts, per_device(): slot_rows = arrived.reshape(-1, width)  13.9 us
    dot_general x1, matrix products, per_device(): jnp.dot(active, w_down[0], preferred_element_type=jnp.float32)  13.3 us
    all_to_all x1, local copies, waits for them, and re-layouts, per_device(): lax.all_to_all(outgoing, 'ep', split_axis=1, concat_axis=1, tiled=True)  11.4 us
  transfers between devices with their start and end apart: 3, of which 3 were waited for; matrix products, arithmetic and copies ran while one was open for 2% of the time, Pallas kernels for 0%

profile of v1, /device:TPU:32, one launch (start us, length us, event | category | flops | bytes accessed | tf_op | source)
XLA Modules:
  0.0 344.8 jit_solution(6986854833559251735)
XLA Ops:
  7.2 0.0 copy-start
  7.2 0.0 reduce-scatter.2.cloned.1.call-start
  7.2 27.5 %all_gather.6 = s32[64,8]{1,0:T(8,128)S(1)} all-gather(s32[8,8]{1,0:T(8,128)} %param.13), channel_id=1, replica_groups=mesh['ep'=32,'gd'=8] {'gd'}, dimensions={0}, use_global_device_ids=true | all-gather | bytes 2304 | tf_op jit(solution)/shard_map/all_gather | solution.py:62
  34.7 0.1 eq.75
  34.8 0.1 copy.29
  34.9 1.4 fusion.55
  36.2 0.1 copy.30
  36.3 0.1 copy.31
  36.4 0.2 fusion.37
  36.6 1.0 fusion.41
  37.6 0.9 fusion.42
  38.5 25.2 %all_gather.7 = bf16[64,4096]{1,0:T(8,128)(2,1)S(1)} all-gather(bf16[8,4096]{1,0:T(8,128)(2,1)S(1)} %fusion.42), channel_id=1, replica_groups=mesh['ep'=32,'gd'=8] {'gd'}, dimensions={0}, use_global_device_ids=true | all-gather | bytes 589824 | tf_op jit(solution)/shard_map/all_gather | solution.py:61
  63.7 1.8 convolution_convert_fusion.1
  65.6 3.4 copy.32
  69.0 80.2 %all_to_all.15 = bf16[8,32,3,4096]{3,0,2,1:T(8,128)(2,1)} all-to-all(bf16[8,32,3,4096]{3,0,2,1:T(8,128)(2,1)S(1)} %bitcast.62), channel_id=1, replica_groups=mesh['ep'=32,'gd'=8] {'ep'}, dimensions={1} | all-to-all | bytes 12582912 | tf_op jit(solution)/shard_map/all_to_all | solution.py:68
  149.2 11.4 %copy.33 = bf16[8,32,3,4096]{3,2,1,0:T(4,128)(2,1)} copy(bf16[8,32,3,4096]{3,0,2,1:T(8,128)(2,1)} %all_to_all.15) | data formatting | bytes 12582912 | tf_op jit(solution)/shard_map/all_to_all | solution.py:68
  160.7 0.0 copy-start.8
  160.7 13.9 %reshape.263 = bf16[768,4096]{1,0:T(8,128)(2,1)} reshape(bf16[8,32,3,4096]{3,2,1,0:T(4,128)(2,1)} %copy.33) | data formatting | bytes 12582912 | tf_op jit(solution)/shard_map/reshape | solution.py:69
  174.5 0.0 copy-done.8
  174.5 5.8 %fusion.4 = f32[768,192]{0,1:T(8,128)} fusion(bf16[768,4096]{1,0:T(8,128)(2,1)} %reshape.263, bf16[1,4096,192]{1,2,0:T(8,128)(2,1)S(1)} %copy-done.8), kind=kOutput, calls=%fused_computation.7 | convolution fusion | flops 1207959552 | bytes 8454144 | tf_op jit(solution)/shard_map/dot_general | solution.py:70
  180.3 0.0 copy-done
  180.3 13.3 %convolution_convert_fusion = bf16[768,4096]{1,0:T(8,128)(2,1)} fusion(bf16[1,192,4096]{2,1,0:T(8,128)(2,1)S(1)} %copy-done, bf16[768,4096]{1,0:T(8,128)(2,1)} %reshape.263, bf16[1,4096,192]{1,2,0:T(8,128)(2,1)} %param.16, f32[768,192]{0,1:T(8,128)} %fusion.4), kind=kOutput, calls=%fused_computation | convolution fusion | flops 2419949568 | bytes 16318464 | tf_op jit(solution)/shard_map/dot_general | solution.py:73
  193.7 0.0 reduce-scatter.2.cloned.1.call-update
  193.7 0.0 copy-start.6
  193.7 0.0 copy-start.7
  193.7 70.1 %reduce-scatter.2.cloned.1.call-done = bf16[96,4096]{1,0:T(8,128)(2,1)} async-done(((bf16[768,4096]{1,0:T(8,128)(2,1)}), bf16[96,4096]{1,0:T(8,128)(2,1)}) %reduce-scatter.2.cloned.1.call-update) | async-done | bytes 786448 | tf_op jit(solution)/shard_map/reduce_scatter | solution.py:76
  263.8 2.8 reshape.272
  266.6 0.0 copy-start.4
  266.6 7.6 %all-to-all-start.1 = ((f32[32,3,4096]{2,1,0:T(4,128)}), f32[32,3,4096]{2,1,0:T(4,128)}, u32[]{:S(2)}, u32[]{:S(2)}) async-start(f32[32,3,4096]{2,1,0:T(4,128)} %reshape.272), calls=%async_computation.2 | async-start | bytes 4194304 | tf_op jit(solution)/shard_map/all_to_all | solution.py:82
  274.2 0.0 copy-done.6
  274.2 0.1 eq.68
  274.3 0.1 fusion.50
  274.4 0.1 reduce_window_sum.22
  274.5 0.2 select_reduce_fusion.1
  274.6 0.1 squeeze_reshape.3
  274.7 0.0 copy-done.7
  274.7 0.1 select_reduce_fusion
  274.8 28.0 %all-to-all-done.1 = f32[32,3,4096]{2,1,0:T(4,128)} async-done(((f32[32,3,4096]{2,1,0:T(4,128)}), f32[32,3,4096]{2,1,0:T(4,128)}, u32[]{:S(2)}, u32[]{:S(2)}) %all-to-all-start.1) | async-done | bytes 1572896 | tf_op jit(solution)/shard_map/all_to_all | solution.py:82
  302.9 2.0 reshape.266
  304.9 0.0 copy-done.4
  304.9 0.8 fusion
  305.8 0.0 copy-start.5
  305.8 0.8 stack.2
  306.6 6.6 %all-to-all-start.2 = ((bf16[8,8,4096]{2,1,0:T(8,128)(2,1)}), bf16[8,8,4096]{2,1,0:T(8,128)(2,1)S(1)}, u32[]{:S(2)}, u32[]{:S(2)}) async-start(bf16[8,8,4096]{2,1,0:T(8,128)(2,1)} %stack.2), calls=%async_computation.3 | async-start | bytes 1048576 | tf_op jit(solution)/shard_map/all_to_all | solution.py:95
  313.2 6.4 %copy.38 = bf16[512,4096]{1,0:T(8,128)(2,1)} copy(bf16[512,4096]{0,1:T(8,128)(2,1)} %bitcast.64) | data formatting | bytes 8388608 | tf_op jit(solution)/shard_map/reshape.116
  319.6 0.0 copy-done.5
  319.6 0.0 copy-done.10
  319.6 0.1 iota_compare_fusion.3
  319.7 9.3 %all-to-all-done.2 = bf16[8,8,4096]{2,1,0:T(8,128)(2,1)S(1)} async-done(((bf16[8,8,4096]{2,1,0:T(8,128)(2,1)}), bf16[8,8,4096]{2,1,0:T(8,128)(2,1)S(1)}, u32[]{:S(2)}, u32[]{:S(2)}) %all-to-all-start.2) | async-done | bytes 524320 | tf_op jit(solution)/shard_map/all_to_all | solution.py:95
  329.0 0.2 fusion.18
  329.2 0.1 rsqrt.22
  329.3 0.0 copy-start.9
  329.3 3.7 %fusion.31 = f32[64,4,128]{2,0,1:T(8,128)S(1)} fusion(bf16[4,128,4096]{2,1,0:T(8,128)(2,1)} %bitcast.63, bf16[8,8,4096]{2,1,0:T(8,128)(2,1)S(1)} %all-to-all-done.2, f32[8,8]{1,0:T(8,128)S(1)} %add_rsqrt_fusion), kind=kOutput, calls=%fused_computation.36 | convolution fusion | flops 269221888 | bytes 4849920 | tf_op jit(solution)/shard_map/dot_general | solution.py:98
  333.1 0.0 copy-done.1
  333.1 0.3 fusion.17
  333.4 0.4 fusion.44
  333.8 0.0 copy-done.2
  333.8 1.8 fusion.56
  335.7 0.2 fusion.47
  335.9 0.0 copy-done.3
  335.9 0.3 fusion.16
  336.3 0.0 copy-done.9
  336.3 1.0 fusion.15
  337.3 0.6 copy.49
  (12 shorter events, 0.1 us)
Async XLA Ops:
  7.2 173.2 %copy-start = (bf16[1,192,4096]{2,1,0:T(8,128)(2,1)S(1)}, bf16[1,192,4096]{2,1,0:T(8,128)(2,1)}, u32[]{:S(2)}) copy-start(bf16[1,192,4096]{2,1,0:T(8,128)(2,1)} %param.17) | copy-start | bytes 4718596
  7.2 256.6 %reduce-scatter.2.cloned.1.call-start = ((), (), s32[]{:S(2)}) async-start(), calls=%async_computation.4 | async-start | bytes 7077888 | tf_op jit(solution)/shard_map/reduce_scatter | solution.py:76
  160.7 13.9 %copy-start.8 = (bf16[1,4096,192]{1,2,0:T(8,128)(2,1)S(1)}, bf16[1,4096,192]{1,2,0:T(8,128)(2,1)}, u32[]{:S(2)}) copy-start(bf16[1,4096,192]{1,2,0:T(8,128)(2,1)} %param.15) | copy-start | bytes 4718596
  193.7 80.5 %copy-start.6 = (s32[8,8]{1,0:T(8,128)S(1)}, s32[8,8]{1,0:T(8,128)}, u32[]{:S(2)}) copy-start(s32[8,8]{1,0:T(8,128)} %param.13) | copy-start | bytes 772
  193.7 81.0 %copy-start.7 = (f32[8,8]{1,0:T(8,128)S(1)}, f32[8,8]{1,0:T(8,128)}, u32[]{:S(2)}) copy-start(f32[8,8]{1,0:T(8,128)} %param.14) | copy-start | bytes 772
  266.6 38.3 %copy-start.4 = (bf16[8,4096]{1,0:T(8,128)(2,1)S(1)}, bf16[8,4096]{1,0:T(8,128)(2,1)}, u32[]{:S(2)}) copy-start(bf16[8,4096]{1,0:T(8,128)(2,1)} %param.12) | copy-start | bytes 196612
  266.6 36.3 %all-to-all-start.1 = ((f32[32,3,4096]{2,1,0:T(4,128)}), f32[32,3,4096]{2,1,0:T(4,128)}, u32[]{:S(2)}, u32[]{:S(2)}) async-start(f32[32,3,4096]{2,1,0:T(4,128)} %reshape.272), calls=%async_computation.2 | async-start | bytes 4194304 | tf_op jit(solution)/shard_map/all_to_all | solution.py:82
  305.8 13.8 %copy-start.5 = (bf16[8,4096]{1,0:T(8,128)(2,1)}, bf16[8,4096]{1,0:T(8,128)(2,1)S(1)}, u32[]{:S(2)}) copy-start(bf16[8,4096]{1,0:T(8,128)(2,1)S(1)} %fusion) | copy-start | bytes 196612
  306.6 22.4 %all-to-all-start.2 = ((bf16[8,8,4096]{2,1,0:T(8,128)(2,1)}), bf16[8,8,4096]{2,1,0:T(8,128)(2,1)S(1)}, u32[]{:S(2)}, u32[]{:S(2)}) async-start(bf16[8,8,4096]{2,1,0:T(8,128)(2,1)} %stack.2), calls=%async_computation.3 | async-start | bytes 1048576 | tf_op jit(solution)/shard_map/all_to_all | solution.py:95
  313.2 6.4 %copy-start.10 = (s32[64]{0:T(128)S(1)}, s32[64]{0:T(128)}, u32[]{:S(2)}) copy-start(s32[64]{0:T(128)} %param.23) | copy-start | bytes 772
  319.6 13.5 %copy-start.1 = (bf16[4096,128]{1,0:T(8,128)(2,1)S(1)}, bf16[4096,128]{1,0:T(8,128)(2,1)}, u32[]{:S(2)}) copy-start(bf16[4096,128]{1,0:T(8,128)(2,1)} %param.19) | copy-start | bytes 3145732
  329.3 4.5 %copy-start.2 = (bf16[64,1,64,128]{3,2,1,0:T(8,128)(2,1)S(1)}, bf16[64,1,64,128]{3,2,1,0:T(8,128)(2,1)}, u32[]{:S(2)}) copy-start(bf16[64,1,64,128]{3,2,1,0:T(8,128)(2,1)} %param.21) | copy-start | bytes 3145732
  329.3 6.6 %copy-start.3 = (bf16[4096,128]{1,0:T(8,128)(2,1)S(1)}, bf16[4096,128]{1,0:T(8,128)(2,1)}, u32[]{:S(2)}) copy-start(bf16[4096,128]{1,0:T(8,128)(2,1)} %param.20) | copy-start | bytes 3145732
  329.3 7.0 %copy-start.9 = (bf16[64,1,64,128]{3,2,1,0:T(8,128)(2,1)S(1)}, bf16[64,1,64,128]{3,2,1,0:T(8,128)(2,1)}, u32[]{:S(2)}) copy-start(bf16[64,1,64,128]{3,2,1,0:T(8,128)(2,1)} %param.22) | copy-start | bytes 3145732
Sparse Core Ops, SparseCore 0:
  193.8 69.9 reduce-scatter.1
